TPU v7x, 32 devices: a whole 2x2x4 slice. The times are simulated.
32 devices in a mesh: gx: 8 (over z, x), gy: 4 (over y, core).
Axes of the slice: x: 2, y: 2, z: 4, core: 2. Of those that a mesh axis runs over, the one named last changes fastest.
Arguments:
- velocity: float32 [3, 128, 128, 256], P(None, 'gx', 'gy'), may hold values from -6 to 6
- owner_block: int32 [65536, 1], P(('gx', 'gy')), may hold values from 0 to 31, as said below
- base_x: int32 [65536], P(('gx', 'gy')), may hold values from 0 to 16
- base_y: int32 [65536], P(('gx', 'gy')), may hold values from 0 to 32
- base_z: int32 [65536], P(('gx', 'gy')), may hold values from 0 to 255
- delta_weights: float32 [12, 65536], P(None, ('gx', 'gy')), may hold values from 0.1 to 1
- marker_offset: float32 [3, 65536], P(None, ('gx', 'gy')), may hold values from -4 to 4
- sphere_motion: float32 [6, 64], P(None, ('gx', 'gy')), may hold values from -6 to 6
- contact_sphere: int32 [128], P(('gx', 'gy')), may hold values from 0 to 63, as said below
- contact_partner: int32 [128], P(('gx', 'gy')), may hold values from 0 to 63
Outputs:
- velocity_star: float32 [3, 128, 128, 256], P(None, 'gx', 'gy')
- new_motion: float32 [6, 64], P(None, ('gx', 'gy'))
Inputs may be any that keep to these rules, and one draw needn't show every extreme that they name: `owner_block`: block b stands at gx index b // 4 and gy index b % 4. Each marker's owner block is the block of the device that holds the marker or one of the eight blocks beside it (periodic along gx, none beyond the walls along gy). Among the markers of one device, at most 256 have any one owner block other than that device's own, and in every device exactly 256 have one such block. `contact_sphere`: entry k names one of the 2 spheres k // 4 * 2 and after, those of the device that holds entry k.
All inputs are finite; a program needn't handle non-finite values.
Results may differ from a plain program's by a relative error of at most 0.0003.
Values sent between devices are 32-bit elements; how exact they have to be, the bound alone decides.
A program may use at most 64 MiB of HBM per device.

v0:
```python
import jax
import jax.numpy as jnp
from jax import lax
from jax.sharding import PartitionSpec as P

ITERS = 4


DIFFUSION = 1.0
RESPONSE = 0.5
DASHPOT = 0.1


def with_halo(array, sides, width):
    for axis, dim in sides:
        size, length = (lax.axis_size(axis), array.shape[dim])
        up = [(i, (i + 1) % size) for i in range(size)]
        down = [(j, i) for i, j in up]
        last = lax.slice_in_dim(array, length - width, length, axis=dim)
        leading = lax.slice_in_dim(array, 0, width, axis=dim)
        before = lax.ppermute(last, axis, up)
        after = lax.ppermute(leading, axis, down)
        array = jnp.concatenate([before, array, after], axis=dim)
    return array


def weight_table(start, weights, extent, wrapped):
    positions = jnp.arange(extent, dtype=jnp.int32)[:, None]
    table = jnp.zeros((extent, start.shape[0]), jnp.float32)
    for offset in range(4):
        target_cell = start + offset
        if wrapped:
            target_cell = target_cell % extent
        table = table + weights[offset][None, :] * (positions == target_cell[None, :]).astype(
            jnp.float32
        )
    return table


def sample_field(field, table_x, table_y, table_z):
    extent_z = field.shape[3]
    partial_z = jnp.dot(field.reshape(-1, extent_z), table_z, precision=lax.Precision.HIGHEST)
    partial_z = partial_z.reshape(3, field.shape[1], field.shape[2], -1)
    partial_y = jnp.sum(partial_z * table_y[None, None, :, :], axis=2)
    return jnp.sum(partial_y * table_x[None, :, :], axis=1)


def deposit_field(forces, table_x, table_y, table_z):
    spread_xy = forces[:, None, None, :] * table_x[None, :, None, :] * table_y[None, None, :, :]
    count = forces.shape[1]
    flat = lax.dot_general(
        spread_xy.reshape(-1, count),
        table_z,
        (((1,), (1,)), ((), ())),
        precision=lax.Precision.HIGHEST,
    )
    return flat.reshape(3, table_x.shape[0], table_y.shape[0], table_z.shape[0])


def wall_mask(row_index, row_count, span_y, margin):
    rows_ext = jnp.arange(span_y + 2 * margin, dtype=jnp.int32)
    global_row = row_index * span_y - margin + rows_ext
    inside = jnp.logical_and(global_row >= 0, global_row < span_y * row_count)
    return inside.astype(jnp.float32)


def faces(state, margin, row_index, row_count):
    grown = with_halo(state, (("gx", 1), ("gy", 2)), margin)
    return grown * wall_mask(row_index, row_count, state.shape[2], margin)[None, None, :, None]


def relax(grown, rhs_part):
    center = grown[:, 1:-1, 1:-1]
    beside_all = grown[:, 2:, 1:-1] + grown[:, :-2, 1:-1] + grown[:, 1:-1, 2:] + grown[:, 1:-1, :-2]
    beside_all = beside_all + jnp.roll(center, -1, 3) + jnp.roll(center, 1, 3)
    return (rhs_part + DIFFUSION * beside_all) / (1.0 + 6.0 * DIFFUSION)


def send_requests(buffer):
    width_rows = buffer.shape[0]
    grown = with_halo(buffer.reshape(width_rows, 3, 3, -1), (("gx", 1), ("gy", 2)), 1)
    return grown[:, 0::2, 0::2].reshape(width_rows, -1)


def send_force_replies(buffer):
    grown = with_halo(buffer.reshape(3, 3, 3, -1), (("gx", 1), ("gy", 2)), 1)
    return grown[:, 0::2, 0::2].reshape(3, -1)


def on_device(
    velocity,
    owner_block,
    base_x,
    base_y,
    base_z,
    delta_weights,
    marker_offset,
    sphere_motion,
    contact_sphere,
    contact_partner,
):
    span_x = velocity.shape[1]
    span_y = velocity.shape[2]
    extent_z = velocity.shape[3]
    row_count = lax.axis_size("gy")
    column_count = lax.axis_size("gx")
    here = lax.axis_index(("gx", "gy"))
    row_index = lax.axis_index("gy")
    column_index = lax.axis_index("gx")
    grown_field = with_halo(velocity, (("gx", 1), ("gy", 2)), 2)
    grown_field = grown_field * wall_mask(row_index, row_count, span_y, 2)[None, None, :, None]
    markers = base_x.shape[0]
    spheres_here = sphere_motion.shape[1]
    per_sphere = markers // spheres_here
    capacity = markers // 8
    owner = owner_block[:, 0]
    at_home = owner == here
    home_weight = at_home.astype(jnp.float32)
    lanes = 9
    step_x = (owner // row_count - column_index + 1 + column_count) % column_count
    step_y = owner % row_count - row_index + 1
    lane = step_x * 3 + step_y
    hits = (lane[:, None] == jnp.arange(lanes, dtype=jnp.int32)[None, :]).astype(jnp.int32)
    hits = hits * (1 - at_home.astype(jnp.int32))[:, None]
    ranked = jnp.sum((jnp.cumsum(hits, axis=0) - hits) * hits, axis=1)
    total_slots = lanes * capacity
    slots = jnp.where(at_home, total_slots, lane * capacity + ranked)
    fetch_slots = jnp.minimum(slots, total_slots - 1)
    linear = sphere_motion[0:3]
    angular = sphere_motion[3:6]
    marker_linear = jnp.broadcast_to(linear[:, :, None], (3, spheres_here, per_sphere)).reshape(
        3, markers
    )
    marker_angular = jnp.broadcast_to(angular[:, :, None], (3, spheres_here, per_sphere)).reshape(
        3, markers
    )
    target = marker_linear + jnp.cross(marker_angular, marker_offset, axis=0)
    coords = jnp.stack([base_x, base_y, base_z]).astype(jnp.float32)
    payload = jnp.concatenate([delta_weights, coords, target], axis=0)
    width_rows = payload.shape[0]
    outgoing = (
        jnp.zeros((width_rows, total_slots), jnp.float32).at[:, slots].set(payload, mode="drop")
    )
    arrived = send_requests(outgoing)
    cell_start = arrived[12:15].astype(jnp.int32)
    start_x = jnp.concatenate([base_x, cell_start[0]])
    start_y = jnp.concatenate([base_y, cell_start[1]])
    start_z = jnp.concatenate([base_z, cell_start[2]])
    weights_all = jnp.concatenate([delta_weights, arrived[0:12]], axis=1)
    table_x = weight_table(start_x, weights_all[0:4], span_x + 4, False)
    table_y = weight_table(start_y, weights_all[4:8], span_y + 4, False)
    table_z = weight_table(start_z, weights_all[8:12], extent_z, True)
    sampled_all = sample_field(grown_field, table_x, table_y, table_z)
    sampled_home = sampled_all[:, :markers]
    sampled = sampled_all[:, markers:]
    slot_force = arrived[15:18] - sampled
    returned = send_force_replies(slot_force)
    force = jnp.where(at_home[None, :], target - sampled_home, returned[:, fetch_slots])
    forces_all = jnp.concatenate([force * home_weight[None, :], slot_force], axis=1)
    spread = deposit_field(forces_all, table_x, table_y, table_z)
    rims = with_halo(spread, (("gx", 1), ("gy", 2)), 2)
    lower = (row_index > 0).astype(jnp.float32)
    upper = (row_index < row_count - 1).astype(jnp.float32)
    source = spread[:, 2 : span_x + 2, 2 : span_y + 2]
    source = source.at[:, 0:2].add(rims[:, 0:2, 4 : span_y + 4])
    source = source.at[:, span_x - 2 :].add(rims[:, span_x + 6 :, 4 : span_y + 4])
    source = source.at[:, :, 0:2].add(lower * rims[:, 4 : span_x + 4, 0:2])
    source = source.at[:, :, span_y - 2 :].add(upper * rims[:, 4 : span_x + 4, span_y + 6 :])
    source = source.at[:, 0:2, 0:2].add(lower * rims[:, 0:2, 0:2])
    source = source.at[:, 0:2, span_y - 2 :].add(upper * rims[:, 0:2, span_y + 6 :])
    source = source.at[:, span_x - 2 :, 0:2].add(lower * rims[:, span_x + 6 :, 0:2])
    source = source.at[:, span_x - 2 :, span_y - 2 :].add(
        upper * rims[:, span_x + 6 :, span_y + 6 :]
    )
    push = jnp.sum(force.reshape(3, spheres_here, per_sphere), axis=-1) / per_sphere
    twist = (
        jnp.sum(
            jnp.cross(marker_offset, force, axis=0).reshape(3, spheres_here, per_sphere), axis=-1
        )
        / per_sphere
    )
    moved = linear - RESPONSE * push
    turned = angular - RESPONSE * twist
    everyone = lax.all_gather(moved, ("gx", "gy"), axis=1, tiled=True)
    all_spheres = everyone.shape[1]
    pick_partner = (
        contact_partner[:, None] == jnp.arange(all_spheres, dtype=jnp.int32)[None, :]
    ).astype(jnp.float32)
    partner_moved = jnp.dot(everyone, pick_partner.T, precision=lax.Precision.HIGHEST)
    local_sphere = contact_sphere - here * spheres_here
    pick_own = (jnp.arange(spheres_here, dtype=jnp.int32)[:, None] == local_sphere[None, :]).astype(
        jnp.float32
    )
    own_moved = jnp.dot(moved, pick_own, precision=lax.Precision.HIGHEST)
    spring = jnp.dot(partner_moved - own_moved, pick_own.T, precision=lax.Precision.HIGHEST)
    settled = moved + DASHPOT * spring
    new_motion = jnp.concatenate([settled, turned], axis=0)
    rhs = velocity + source
    state = rhs
    for sweep in range(ITERS):
        grown = faces(state, 1, row_index, row_count)
        state = relax(grown, rhs)
    return (state, new_motion)


def solution(mesh):
    placed = (
        P(None, "gx", "gy", None),
        P(("gx", "gy"), None),
        P(("gx", "gy")),
        P(("gx", "gy")),
        P(("gx", "gy")),
        P(None, ("gx", "gy")),
        P(None, ("gx", "gy")),
        P(None, ("gx", "gy")),
        P(("gx", "gy")),
        P(("gx", "gy")),
    )
    return jax.shard_map(
        on_device,
        mesh=mesh,
        in_specs=placed,
        out_specs=(P(None, "gx", "gy", None), P(None, ("gx", "gy"))),
        check_vma=False,
    )
```

profile of v0, /device:TPU:0, one launch (start us, length us, event | category | flops | bytes accessed | tf_op | source)
XLA Modules:
  0.0 269.5 jit_solution(14954151166112825855)
XLA Ops:
  0.7 1.8 fusion.96
  2.5 6.0 %collective-permute-start.1 = (f32[3,2,32,256]{3,2,1,0:T(8,128)S(1)}, f32[3,2,32,256]{3,2,1,0:T(8,128)S(1)}, u32[]{:S(2)}, u32[]{:S(2)}) collective-permute-start(f32[3,2,32,256]{3,2,1,0:T(8,128)S(1)} %get-tuple-element.153), channel_id=1, source_target_pairs={{4,0},{8,4},{12,8},{16,12},{20,16},{24,20},{28,24},{0,28},{5,1},{9... | collective-permute-start | bytes 589832 | tf_op jit(solution)/shard_map/ppermute | solution.py:22
  10.5 2.6 reduce-window.6
  14.5 5.9 %scatter_custom_fusion = f32[18,2304]{0,1:T(8,128)S(1)} fusion(s32[2048]{0:T(1024)S(1)} %bitcast.93, f32[2048,18]{1,0:T(8,128)S(1)} %copy.59, f32[]{:T(128)} %constant.344.clone.1), kind=kCustom, calls=%fused_computation.81 | custom fusion | bytes 165892 | tf_op jit(solution)/shard_map/scatter | solution.py:142
  21.0 4.8 %collective-permute-start.5 = (f32[18,1,3,256]{3,2,1,0:T(4,128)S(1)}, f32[18,1,3,256]{3,2,1,0:T(4,128)S(1)}, u32[]{:S(2)}, u32[]{:S(2)}) collective-permute-start(f32[18,1,3,256]{3,2,1,0:T(4,128)S(1)} %get-tuple-element.160), channel_id=1, source_target_pairs={{4,0},{8,4},{12,8},{16,12},{20,16},{24,20},{28,24},{0,28},{5,1},{9... | collective-permute-start | bytes 165896 | tf_op jit(solution)/shard_map/ppermute | solution.py:22
  28.6 1.7 collective-permute-start.7
  32.8 1.9 slice.648
  40.8 2.0 collective-permute-done.2
  43.7 46.3 %multiply_reduce_fusion = f32[3,20,4352]{2,1,0:T(8,128)S(1)} fusion(f32[36,4352]{1,0:T(8,128)S(1)} %select_add_fusion.3, f32[4352]{0:T(1024)S(1)} %get-tuple-element.107, s32[4352]{0:T(1024)S(1)} %get-tuple-element.180, f32[4352]{0:T(1024)S(1)} %get-tuple-element.108, s32[4352]{0:T(1024)S(1)} %get-tuple-element.179, f32[4352]{0:T(1024)S(1)} %get-tuple-element.109, ...), kind=kOutput, calls=%fused_computation.4 | convolution fusion | flops 28908576768 | bytes 4022272 | tf_op jit(solution)/shard_map/dot_general | solution.py:42
  91.1 4.5 %collective-permute-start.9 = (f32[3,1,3,256]{3,2,1,0:T(4,128)S(1)}, f32[3,1,3,256]{3,2,1,0:T(4,128)S(1)}, u32[]{:S(2)}, u32[]{:S(2)}) collective-permute-start(f32[3,1,3,256]{3,2,1,0:T(4,128)S(1)} %get-tuple-element.169), channel_id=1, source_target_pairs={{4,0},{8,4},{12,8},{16,12},{20,16},{24,20},{28,24},{0,28},{5,1},{9... | collective-permute-start | bytes 27656 | tf_op jit(solution)/shard_map/ppermute | solution.py:22
  98.9 3.6 %fusion.114 = f32[256,4352,1,1]{1,0,3,2:T(8,128)} fusion(f32[4352]{0:T(1024)S(1)} %get-tuple-element.107, s32[4352]{0:T(1024)S(1)} %get-tuple-element.180, f32[4352]{0:T(1024)S(1)} %get-tuple-element.108, s32[4352]{0:T(1024)S(1)} %get-tuple-element.179, f32[4352]{0:T(1024)S(1)} %get-tuple-element.109, s32[4352]{0:T(1024)S(1)} %get-tuple-element.178, ...), kind=kLoop, calls=%fused_computation.7.clone.2 | loop fusion | flops 12255232 | bytes 4595712 | tf_op jit(solution)/shard_map/dot_general | solution.py:51
  103.2 5.5 %gather_fusion = f32[2048,3]{1,0:T(8,128)S(1)} fusion(f32[3,2304]{0,1:T(8,128)S(1)} %bitcast.73, s32[2048]{0:T(1024)S(1)} %copy-done.11), kind=kCustom, calls=%fused_computation | custom fusion | bytes 57344 | tf_op jit(solution)/shard_map/gather | solution.py:158
  109.8 35.5 %fusion = f32[3,20,36,256]{3,2,1,0:T(8,128)S(1)} fusion(f32[3,20,4352]{2,1,0:T(8,128)S(1)} %broadcast_multiply_fusion, f32[36,4352]{1,0:T(8,128)S(1)} %copy-done.2, f32[256,4352,1,1]{1,0,3,2:T(8,128)} %fusion.114), kind=kOutput, calls=%fused_computation.2 | convolution fusion | flops 28887183360 | bytes 8339456 | tf_op jit(solution)/shard_map/dot_general | solution.py:51
  145.3 5.0 %collective-permute-start.13 = (f32[3,2,36,256]{3,2,1,0:T(8,128)S(1)}, f32[3,2,36,256]{3,2,1,0:T(8,128)S(1)}, u32[]{:S(2)}, u32[]{:S(2)}) collective-permute-start(f32[3,2,36,256]{3,2,1,0:T(8,128)S(1)} %get-tuple-element.117), channel_id=1, source_target_pairs={{4,0},{8,4},{12,8},{16,12},{20,16},{24,20},{28,24},{0,28},{5,1},{9... | collective-permute-start | bytes 663560 | tf_op jit(solution)/shard_map/ppermute | solution.py:22
  150.8 4.8 %collective-permute-done.13 = f32[3,2,36,256]{3,2,1,0:T(8,128)S(1)} collective-permute-done((f32[3,2,36,256]{3,2,1,0:T(8,128)S(1)}, f32[3,2,36,256]{3,2,1,0:T(8,128)S(1)}, u32[]{:S(2)}, u32[]{:S(2)}) %collective-permute-start.13) | collective-permute-done | bytes 221216 | tf_op jit(solution)/shard_map/ppermute | solution.py:22
  155.6 5.1 %collective-permute-done.12 = f32[3,2,36,256]{3,2,1,0:T(8,128)S(1)} collective-permute-done((f32[3,2,36,256]{3,2,1,0:T(8,128)S(1)}, f32[3,2,36,256]{3,2,1,0:T(8,128)S(1)}, u32[]{:S(2)}, u32[]{:S(2)}) %collective-permute-start.12) | collective-permute-done | bytes 221216 | tf_op jit(solution)/shard_map/ppermute | solution.py:21
  161.4 4.7 %collective-permute-done.14 = f32[3,24,2,256]{3,2,1,0:T(2,128)S(1)} collective-permute-done((f32[3,24,2,256]{3,2,1,0:T(2,128)S(1)}, f32[3,24,2,256]{3,2,1,0:T(2,128)S(1)}, u32[]{:S(2)}, u32[]{:S(2)}) %collective-permute-start.14) | collective-permute-done | bytes 147488 | tf_op jit(solution)/shard_map/ppermute | solution.py:21
  166.4 2.0 add_select_fusion.4
  171.8 4.7 %collective-permute-start.17 = (f32[3,1,32,256]{3,2,1,0:T(8,128)S(1)}, f32[3,1,32,256]{3,2,1,0:T(8,128)S(1)}, u32[]{:S(2)}, u32[]{:S(2)}) collective-permute-start(f32[3,1,32,256]{3,2,1,0:T(8,128)S(1)} %get-tuple-element.152), channel_id=1, source_target_pairs={{4,0},{8,4},{12,8},{16,12},{20,16},{24,20},{28,24},{0,28},{5,1},{9... | collective-permute-start | bytes 294920 | tf_op jit(solution)/shard_map/ppermute | solution.py:22
  176.5 2.6 collective-permute-done.16
  179.2 1.7 collective-permute-start.19
  181.0 1.8 collective-permute-done.18
  185.9 4.7 %collective-permute-start.21 = (f32[3,1,32,256]{3,2,1,0:T(8,128)S(1)}, f32[3,1,32,256]{3,2,1,0:T(8,128)S(1)}, u32[]{:S(2)}, u32[]{:S(2)}) collective-permute-start(f32[3,1,32,256]{3,2,1,0:T(8,128)S(1)} %get-tuple-element.150), channel_id=1, source_target_pairs={{4,0},{8,4},{12,8},{16,12},{20,16},{24,20},{28,24},{0,28},{5,1},{9... | collective-permute-start | bytes 294920 | tf_op jit(solution)/shard_map/ppermute | solution.py:22
  191.1 2.5 collective-permute-done.20
  195.8 42.0 %all-gather = f32[32,2,3]{2,1,0:T(2,128)S(1)} all-gather(f32[1,2,3]{2,1,0:T(2,128)S(1)} %get-tuple-element.186), channel_id=1, replica_groups=mesh['gx'=8,'gy'=4] {'gx','gy'}, dimensions={0}, use_global_device_ids=true | all-gather | bytes 792 | tf_op jit(solution)/shard_map/all_gather | solution.py:184
  240.3 4.7 %collective-permute-start.25 = (f32[3,1,32,256]{3,2,1,0:T(8,128)S(1)}, f32[3,1,32,256]{3,2,1,0:T(8,128)S(1)}, u32[]{:S(2)}, u32[]{:S(2)}) collective-permute-start(f32[3,1,32,256]{3,2,1,0:T(8,128)S(1)} %get-tuple-element.148), channel_id=1, source_target_pairs={{4,0},{8,4},{12,8},{16,12},{20,16},{24,20},{28,24},{0,28},{5,1},{9... | collective-permute-start | bytes 294920 | tf_op jit(solution)/shard_map/ppermute | solution.py:22
  245.2 2.8 %collective-permute-done.24 = f32[3,1,32,256]{3,2,1,0:T(8,128)S(1)} collective-permute-done((f32[3,1,32,256]{3,2,1,0:T(8,128)S(1)}, f32[3,1,32,256]{3,2,1,0:T(8,128)S(1)}, u32[]{:S(2)}, u32[]{:S(2)}) %collective-permute-start.24) | collective-permute-done | bytes 98336 | tf_op jit(solution)/shard_map/ppermute | solution.py:21
  250.1 2.0 collective-permute-done.26
  254.6 4.7 %collective-permute-start.29 = (f32[3,1,32,256]{3,2,1,0:T(8,128)S(1)}, f32[3,1,32,256]{3,2,1,0:T(8,128)S(1)}, u32[]{:S(2)}, u32[]{:S(2)}) collective-permute-start(f32[3,1,32,256]{3,2,1,0:T(8,128)S(1)} %get-tuple-element.146), channel_id=1, source_target_pairs={{4,0},{8,4},{12,8},{16,12},{20,16},{24,20},{28,24},{0,28},{5,1},{9... | collective-permute-start | bytes 294920 | tf_op jit(solution)/shard_map/ppermute | solution.py:22
  259.4 2.5 collective-permute-done.28
  262.0 1.7 collective-permute-start.31
  267.2 2.1 fusion.31
  (211 shorter events, 43.5 us)
Async XLA Ops:
  2.5 35.7 %collective-permute-start.1 = (f32[3,2,32,256]{3,2,1,0:T(8,128)S(1)}, f32[3,2,32,256]{3,2,1,0:T(8,128)S(1)}, u32[]{:S(2)}, u32[]{:S(2)}) collective-permute-start(f32[3,2,32,256]{3,2,1,0:T(8,128)S(1)} %get-tuple-element.153), channel_id=1, source_target_pairs={{4,0},{8,4},{12,8},{16,12},{20,16},{24,20},{28,24},{0,28},{5,1},{9... | collective-permute-start | bytes 589832 | tf_op jit(solution)/shard_map/ppermute | solution.py:22
  8.5 29.5 %collective-permute-start = (f32[3,2,32,256]{3,2,1,0:T(8,128)}, f32[3,2,32,256]{3,2,1,0:T(8,128)S(1)}, u32[]{:S(2)}, u32[]{:S(2)}) collective-permute-start(f32[3,2,32,256]{3,2,1,0:T(8,128)} %get-tuple-element.154), channel_id=1, source_target_pairs={{0,4},{4,8},{8,12},{12,16},{16,20},{20,24},{24,28},{28,0},{1,5},{5... | collective-permute-start | bytes 589832 | tf_op jit(solution)/shard_map/ppermute | solution.py:21
  20.9 7.5 %collective-permute-start.4 = (f32[18,1,3,256]{3,2,1,0:T(4,128)S(1)}, f32[18,1,3,256]{3,2,1,0:T(4,128)S(1)}, u32[]{:S(2)}, u32[]{:S(2)}) collective-permute-start(f32[18,1,3,256]{3,2,1,0:T(4,128)S(1)} %get-tuple-element.159), channel_id=1, source_target_pairs={{0,4},{4,8},{8,12},{12,16},{16,20},{20,24},{24,28},{28,0},{1,5},{5... | collective-permute-start | bytes 165896 | tf_op jit(solution)/shard_map/ppermute | solution.py:21
  21.0 7.4 %collective-permute-start.5 = (f32[18,1,3,256]{3,2,1,0:T(4,128)S(1)}, f32[18,1,3,256]{3,2,1,0:T(4,128)S(1)}, u32[]{:S(2)}, u32[]{:S(2)}) collective-permute-start(f32[18,1,3,256]{3,2,1,0:T(4,128)S(1)} %get-tuple-element.160), channel_id=1, source_target_pairs={{4,0},{8,4},{12,8},{16,12},{20,16},{24,20},{28,24},{0,28},{5,1},{9... | collective-permute-start | bytes 165896 | tf_op jit(solution)/shard_map/ppermute | solution.py:22
  28.5 4.0 %collective-permute-start.6 = (f32[18,5,1,256]{3,2,1,0:T(1,128)S(1)}, f32[18,5,1,256]{3,2,1,0:T(1,128)S(1)}, u32[]{:S(2)}, u32[]{:S(2)}) collective-permute-start(f32[18,5,1,256]{3,2,1,0:T(1,128)S(1)} %get-tuple-element.155), channel_id=1, source_target_pairs={{0,1},{1,2},{2,3},{3,0},{4,5},{5,6},{6,7},{7,4},{8,9},{9,10},{10,1... | collective-permute-start | bytes 276488 | tf_op jit(solution)/shard_map/ppermute | solution.py:21
  28.6 4.0 %collective-permute-start.7 = (f32[18,5,1,256]{3,2,1,0:T(1,128)S(1)}, f32[18,5,1,256]{3,2,1,0:T(1,128)S(1)}, u32[]{:S(2)}, u32[]{:S(2)}) collective-permute-start(f32[18,5,1,256]{3,2,1,0:T(1,128)S(1)} %get-tuple-element.156), channel_id=1, source_target_pairs={{1,0},{2,1},{3,2},{0,3},{5,4},{6,5},{7,6},{4,7},{9,8},{10,9},{11,1... | collective-permute-start | bytes 276488 | tf_op jit(solution)/shard_map/ppermute | solution.py:22
  38.3 4.5 %collective-permute-start.2 = (f32[3,20,2,256]{3,2,1,0:T(2,128)S(1)}, f32[3,20,2,256]{3,2,1,0:T(2,128)S(1)}, u32[]{:S(2)}, u32[]{:S(2)}) collective-permute-start(f32[3,20,2,256]{3,2,1,0:T(2,128)S(1)} %get-tuple-element.135), channel_id=1, source_target_pairs={{0,1},{1,2},{2,3},{3,0},{4,5},{5,6},{6,7},{7,4},{8,9},{9,10},{10,1... | collective-permute-start | bytes 368648 | tf_op jit(solution)/shard_map/ppermute | solution.py:21
  39.9 3.3 %collective-permute-start.3 = (f32[3,20,2,256]{3,2,1,0:T(2,128)S(1)}, f32[3,20,2,256]{3,2,1,0:T(2,128)S(1)}, u32[]{:S(2)}, u32[]{:S(2)}) collective-permute-start(f32[3,20,2,256]{3,2,1,0:T(2,128)S(1)} %get-tuple-element.136), channel_id=1, source_target_pairs={{1,0},{2,1},{3,2},{0,3},{5,4},{6,5},{7,6},{4,7},{9,8},{10,9},{11,1... | collective-permute-start | bytes 368648 | tf_op jit(solution)/shard_map/ppermute | solution.py:22
  90.3 6.4 %collective-permute-start.8 = (f32[3,1,3,256]{3,2,1,0:T(4,128)S(1)}, f32[3,1,3,256]{3,2,1,0:T(4,128)S(1)}, u32[]{:S(2)}, u32[]{:S(2)}) collective-permute-start(f32[3,1,3,256]{3,2,1,0:T(4,128)S(1)} %get-tuple-element.170), channel_id=1, source_target_pairs={{0,4},{4,8},{8,12},{12,16},{16,20},{20,24},{24,28},{28,0},{1,5},{5... | collective-permute-start | bytes 27656 | tf_op jit(solution)/shard_map/ppermute | solution.py:21
  91.1 5.9 %collective-permute-start.9 = (f32[3,1,3,256]{3,2,1,0:T(4,128)S(1)}, f32[3,1,3,256]{3,2,1,0:T(4,128)S(1)}, u32[]{:S(2)}, u32[]{:S(2)}) collective-permute-start(f32[3,1,3,256]{3,2,1,0:T(4,128)S(1)} %get-tuple-element.169), channel_id=1, source_target_pairs={{4,0},{8,4},{12,8},{16,12},{20,16},{24,20},{28,24},{0,28},{5,1},{9... | collective-permute-start | bytes 27656 | tf_op jit(solution)/shard_map/ppermute | solution.py:22
  97.1 5.5 %collective-permute-start.10 = (f32[3,5,1,256]{3,2,1,0:T(1,128)S(1)}, f32[3,5,1,256]{3,2,1,0:T(1,128)S(1)}, u32[]{:S(2)}, u32[]{:S(2)}) collective-permute-start(f32[3,5,1,256]{3,2,1,0:T(1,128)S(1)} %get-tuple-element.167), channel_id=1, source_target_pairs={{0,1},{1,2},{2,3},{3,0},{4,5},{5,6},{6,7},{7,4},{8,9},{9,10},{10,1... | collective-permute-start | bytes 46088 | tf_op jit(solution)/shard_map/ppermute | solution.py:21
  97.9 4.7 %collective-permute-start.11 = (f32[3,5,1,256]{3,2,1,0:T(1,128)S(1)}, f32[3,5,1,256]{3,2,1,0:T(1,128)S(1)}, u32[]{:S(2)}, u32[]{:S(2)}) collective-permute-start(f32[3,5,1,256]{3,2,1,0:T(1,128)S(1)} %get-tuple-element.168), channel_id=1, source_target_pairs={{1,0},{2,1},{3,2},{0,3},{5,4},{6,5},{7,6},{4,7},{9,8},{10,9},{11,1... | collective-permute-start | bytes 46088 | tf_op jit(solution)/shard_map/ppermute | solution.py:22
  145.3 10.2 %collective-permute-start.13 = (f32[3,2,36,256]{3,2,1,0:T(8,128)S(1)}, f32[3,2,36,256]{3,2,1,0:T(8,128)S(1)}, u32[]{:S(2)}, u32[]{:S(2)}) collective-permute-start(f32[3,2,36,256]{3,2,1,0:T(8,128)S(1)} %get-tuple-element.117), channel_id=1, source_target_pairs={{4,0},{8,4},{12,8},{16,12},{20,16},{24,20},{28,24},{0,28},{5,1},{9... | collective-permute-start | bytes 663560 | tf_op jit(solution)/shard_map/ppermute | solution.py:22
  150.4 10.3 %collective-permute-start.12 = (f32[3,2,36,256]{3,2,1,0:T(8,128)S(1)}, f32[3,2,36,256]{3,2,1,0:T(8,128)S(1)}, u32[]{:S(2)}, u32[]{:S(2)}) collective-permute-start(f32[3,2,36,256]{3,2,1,0:T(8,128)S(1)} %get-tuple-element.118), channel_id=1, source_target_pairs={{0,4},{4,8},{8,12},{12,16},{16,20},{20,24},{24,28},{28,0},{1,5},{5... | collective-permute-start | bytes 663560 | tf_op jit(solution)/shard_map/ppermute | solution.py:21
  160.8 5.4 %collective-permute-start.15 = (f32[3,24,2,256]{3,2,1,0:T(2,128)S(1)}, f32[3,24,2,256]{3,2,1,0:T(2,128)S(1)}, u32[]{:S(2)}, u32[]{:S(2)}) collective-permute-start(f32[3,24,2,256]{3,2,1,0:T(2,128)S(1)} %get-tuple-element.115), channel_id=1, source_target_pairs={{1,0},{2,1},{3,2},{0,3},{5,4},{6,5},{7,6},{4,7},{9,8},{10,9},{11,1... | collective-permute-start | bytes 442376 | tf_op jit(solution)/shard_map/ppermute | solution.py:22
  160.8 5.3 %collective-permute-start.14 = (f32[3,24,2,256]{3,2,1,0:T(2,128)S(1)}, f32[3,24,2,256]{3,2,1,0:T(2,128)S(1)}, u32[]{:S(2)}, u32[]{:S(2)}) collective-permute-start(f32[3,24,2,256]{3,2,1,0:T(2,128)S(1)} %get-tuple-element.116), channel_id=1, source_target_pairs={{0,1},{1,2},{2,3},{3,0},{4,5},{5,6},{6,7},{7,4},{8,9},{9,10},{10,1... | collective-permute-start | bytes 442376 | tf_op jit(solution)/shard_map/ppermute | solution.py:21
  171.7 7.4 %collective-permute-start.16 = (f32[3,1,32,256]{3,2,1,0:T(8,128)S(1)}, f32[3,1,32,256]{3,2,1,0:T(8,128)S(1)}, u32[]{:S(2)}, u32[]{:S(2)}) collective-permute-start(f32[3,1,32,256]{3,2,1,0:T(8,128)S(1)} %get-tuple-element.151), channel_id=1, source_target_pairs={{0,4},{4,8},{8,12},{12,16},{16,20},{20,24},{24,28},{28,0},{1,5},{5... | collective-permute-start | bytes 294920 | tf_op jit(solution)/shard_map/ppermute | solution.py:21
  171.8 7.3 %collective-permute-start.17 = (f32[3,1,32,256]{3,2,1,0:T(8,128)S(1)}, f32[3,1,32,256]{3,2,1,0:T(8,128)S(1)}, u32[]{:S(2)}, u32[]{:S(2)}) collective-permute-start(f32[3,1,32,256]{3,2,1,0:T(8,128)S(1)} %get-tuple-element.152), channel_id=1, source_target_pairs={{4,0},{8,4},{12,8},{16,12},{20,16},{24,20},{28,24},{0,28},{5,1},{9... | collective-permute-start | bytes 294920 | tf_op jit(solution)/shard_map/ppermute | solution.py:22
  179.2 3.6 %collective-permute-start.18 = (f32[3,18,1,256]{3,2,1,0:T(1,128)S(1)}, f32[3,18,1,256]{3,2,1,0:T(1,128)S(1)}, u32[]{:S(2)}, u32[]{:S(2)}) collective-permute-start(f32[3,18,1,256]{3,2,1,0:T(1,128)S(1)} %get-tuple-element.143), channel_id=1, source_target_pairs={{0,1},{1,2},{2,3},{3,0},{4,5},{5,6},{6,7},{7,4},{8,9},{9,10},{10,1... | collective-permute-start | bytes 165896 | tf_op jit(solution)/shard_map/ppermute | solution.py:21
  179.2 3.6 %collective-permute-start.19 = (f32[3,18,1,256]{3,2,1,0:T(1,128)S(1)}, f32[3,18,1,256]{3,2,1,0:T(1,128)S(1)}, u32[]{:S(2)}, u32[]{:S(2)}) collective-permute-start(f32[3,18,1,256]{3,2,1,0:T(1,128)S(1)} %get-tuple-element.144), channel_id=1, source_target_pairs={{1,0},{2,1},{3,2},{0,3},{5,4},{6,5},{7,6},{4,7},{9,8},{10,9},{11,1... | collective-permute-start | bytes 165896 | tf_op jit(solution)/shard_map/ppermute | solution.py:22
  185.9 7.7 %collective-permute-start.20 = (f32[3,1,32,256]{3,2,1,0:T(8,128)}, f32[3,1,32,256]{3,2,1,0:T(8,128)S(1)}, u32[]{:S(2)}, u32[]{:S(2)}) collective-permute-start(f32[3,1,32,256]{3,2,1,0:T(8,128)} %get-tuple-element.149), channel_id=1, source_target_pairs={{0,4},{4,8},{8,12},{12,16},{16,20},{20,24},{24,28},{28,0},{1,5},{5... | collective-permute-start | bytes 294920 | tf_op jit(solution)/shard_map/ppermute | solution.py:21
  185.9 7.7 %collective-permute-start.21 = (f32[3,1,32,256]{3,2,1,0:T(8,128)S(1)}, f32[3,1,32,256]{3,2,1,0:T(8,128)S(1)}, u32[]{:S(2)}, u32[]{:S(2)}) collective-permute-start(f32[3,1,32,256]{3,2,1,0:T(8,128)S(1)} %get-tuple-element.150), channel_id=1, source_target_pairs={{4,0},{8,4},{12,8},{16,12},{20,16},{24,20},{28,24},{0,28},{5,1},{9... | collective-permute-start | bytes 294920 | tf_op jit(solution)/shard_map/ppermute | solution.py:22
  193.7 44.2 %collective-permute-start.22 = (f32[3,18,1,256]{3,2,1,0:T(1,128)S(1)}, f32[3,18,1,256]{3,2,1,0:T(1,128)S(1)}, u32[]{:S(2)}, u32[]{:S(2)}) collective-permute-start(f32[3,18,1,256]{3,2,1,0:T(1,128)S(1)} %get-tuple-element.141), channel_id=1, source_target_pairs={{0,1},{1,2},{2,3},{3,0},{4,5},{5,6},{6,7},{7,4},{8,9},{9,10},{10,1... | collective-permute-start | bytes 165896 | tf_op jit(solution)/shard_map/ppermute | solution.py:21
  194.4 43.5 %collective-permute-start.23 = (f32[3,18,1,256]{3,2,1,0:T(1,128)S(1)}, f32[3,18,1,256]{3,2,1,0:T(1,128)S(1)}, u32[]{:S(2)}, u32[]{:S(2)}) collective-permute-start(f32[3,18,1,256]{3,2,1,0:T(1,128)S(1)} %get-tuple-element.142), channel_id=1, source_target_pairs={{1,0},{2,1},{3,2},{0,3},{5,4},{6,5},{7,6},{4,7},{9,8},{10,9},{11,1... | collective-permute-start | bytes 165896 | tf_op jit(solution)/shard_map/ppermute | solution.py:22
  240.3 7.8 %collective-permute-start.24 = (f32[3,1,32,256]{3,2,1,0:T(8,128)S(1)}, f32[3,1,32,256]{3,2,1,0:T(8,128)S(1)}, u32[]{:S(2)}, u32[]{:S(2)}) collective-permute-start(f32[3,1,32,256]{3,2,1,0:T(8,128)S(1)} %get-tuple-element.147), channel_id=1, source_target_pairs={{0,4},{4,8},{8,12},{12,16},{16,20},{20,24},{24,28},{28,0},{1,5},{5... | collective-permute-start | bytes 294920 | tf_op jit(solution)/shard_map/ppermute | solution.py:21
  240.3 7.7 %collective-permute-start.25 = (f32[3,1,32,256]{3,2,1,0:T(8,128)S(1)}, f32[3,1,32,256]{3,2,1,0:T(8,128)S(1)}, u32[]{:S(2)}, u32[]{:S(2)}) collective-permute-start(f32[3,1,32,256]{3,2,1,0:T(8,128)S(1)} %get-tuple-element.148), channel_id=1, source_target_pairs={{4,0},{8,4},{12,8},{16,12},{20,16},{24,20},{28,24},{0,28},{5,1},{9... | collective-permute-start | bytes 294920 | tf_op jit(solution)/shard_map/ppermute | solution.py:22
  248.1 4.0 %collective-permute-start.26 = (f32[3,18,1,256]{3,2,1,0:T(1,128)S(1)}, f32[3,18,1,256]{3,2,1,0:T(1,128)S(1)}, u32[]{:S(2)}, u32[]{:S(2)}) collective-permute-start(f32[3,18,1,256]{3,2,1,0:T(1,128)S(1)} %get-tuple-element.139), channel_id=1, source_target_pairs={{0,1},{1,2},{2,3},{3,0},{4,5},{5,6},{6,7},{7,4},{8,9},{9,10},{10,1... | collective-permute-start | bytes 165896 | tf_op jit(solution)/shard_map/ppermute | solution.py:21
  248.2 3.9 %collective-permute-start.27 = (f32[3,18,1,256]{3,2,1,0:T(1,128)S(1)}, f32[3,18,1,256]{3,2,1,0:T(1,128)S(1)}, u32[]{:S(2)}, u32[]{:S(2)}) collective-permute-start(f32[3,18,1,256]{3,2,1,0:T(1,128)S(1)} %get-tuple-element.140), channel_id=1, source_target_pairs={{1,0},{2,1},{3,2},{0,3},{5,4},{6,5},{7,6},{4,7},{9,8},{10,9},{11,1... | collective-permute-start | bytes 165896 | tf_op jit(solution)/shard_map/ppermute | solution.py:22
  254.5 7.4 %collective-permute-start.28 = (f32[3,1,32,256]{3,2,1,0:T(8,128)S(1)}, f32[3,1,32,256]{3,2,1,0:T(8,128)S(1)}, u32[]{:S(2)}, u32[]{:S(2)}) collective-permute-start(f32[3,1,32,256]{3,2,1,0:T(8,128)S(1)} %get-tuple-element.145), channel_id=1, source_target_pairs={{0,4},{4,8},{8,12},{12,16},{16,20},{20,24},{24,28},{28,0},{1,5},{5... | collective-permute-start | bytes 294920 | tf_op jit(solution)/shard_map/ppermute | solution.py:21
  254.6 7.3 %collective-permute-start.29 = (f32[3,1,32,256]{3,2,1,0:T(8,128)S(1)}, f32[3,1,32,256]{3,2,1,0:T(8,128)S(1)}, u32[]{:S(2)}, u32[]{:S(2)}) collective-permute-start(f32[3,1,32,256]{3,2,1,0:T(8,128)S(1)} %get-tuple-element.146), channel_id=1, source_target_pairs={{4,0},{8,4},{12,8},{16,12},{20,16},{24,20},{28,24},{0,28},{5,1},{9... | collective-permute-start | bytes 294920 | tf_op jit(solution)/shard_map/ppermute | solution.py:22
  262.0 3.8 %collective-permute-start.30 = (f32[3,18,1,256]{3,2,1,0:T(1,128)S(1)}, f32[3,18,1,256]{3,2,1,0:T(1,128)S(1)}, u32[]{:S(2)}, u32[]{:S(2)}) collective-permute-start(f32[3,18,1,256]{3,2,1,0:T(1,128)S(1)} %get-tuple-element.137), channel_id=1, source_target_pairs={{0,1},{1,2},{2,3},{3,0},{4,5},{5,6},{6,7},{7,4},{8,9},{9,10},{10,1... | collective-permute-start | bytes 165896 | tf_op jit(solution)/shard_map/ppermute | solution.py:21
  262.0 3.7 %collective-permute-start.31 = (f32[3,18,1,256]{3,2,1,0:T(1,128)S(1)}, f32[3,18,1,256]{3,2,1,0:T(1,128)S(1)}, u32[]{:S(2)}, u32[]{:S(2)}) collective-permute-start(f32[3,18,1,256]{3,2,1,0:T(1,128)S(1)} %get-tuple-element.138), channel_id=1, source_target_pairs={{1,0},{2,1},{3,2},{0,3},{5,4},{6,5},{7,6},{4,7},{9,8},{10,9},{11,1... | collective-permute-start | bytes 165896 | tf_op jit(solution)/shard_map/ppermute | solution.py:22
  (20 other events, 187.3 us)
where the time goes:
time: 275 us; the launch traced here: 270 us
  matrix products  82.3 us (30%)
  starting transfers between devices  53.7 us (20%)
  blocking collectives  42 us (15%)
  waiting for transfers between devices  35.6 us (13%)
  local copies, waits for them, and re-layouts  30.2 us (11%)
  other arithmetic  23.9 us (9%)
    ppermute x16, starting transfers between devices, with_halo(): after = lax.ppermute(leading, axis, down)  49.3 us
    dot_general x1, matrix products, sample_field(): jnp.dot(field.reshape(-1, extent_z), table_z, precision=lax.Precision.HIG...  46.3 us
    all_gather x1, blocking collectives, on_device(): everyone = lax.all_gather(moved, ('gx', 'gy'), axis=1, tiled=True)  42 us
    dot_general x1, matrix products, deposit_field(): lax.dot_general(spread_xy.reshape(-1, count), table_z, (((1,), (1,)), (()...  35.5 us
    ppermute x16, waiting for transfers between devices, with_halo(): before = lax.ppermute(last, axis, up)  30.1 us
    scatter x1, local copies, waits for them, and re-layouts, on_device(): jnp.zeros((width_rows, total_slots), jnp.float32).at[:, slots]  5.89 us
    gather x2, local copies, waits for them, and re-layouts, on_device(): returned[:, fetch_slots]  5.79 us
    another operation x6, other arithmetic  5.64 us
  transfers between devices with their start and end apart: 32, of which 15 were waited for; matrix products, arithmetic and copies ran while one was open for 10% of the time, Pallas kernels for 0%

commit v1 on v0

v1 whole, which is shorter than its diff:
```python
import functools

import jax
import jax.numpy as jnp
import numpy as np
from jax import lax
from jax.experimental import pallas as pl
from jax.experimental.pallas import tpu as pltpu
from jax.sharding import PartitionSpec as P

ITERS = 4


DIFFUSION = 1.0
RESPONSE = 0.5
DASHPOT = 0.1
TILE_ROWS = 16
TILE_LANES = 128


def shift(array, axis, step, periodic):
    size = lax.axis_size(axis)
    pairs = [(i, (i + step) % size) for i in range(size) if periodic or 0 <= i + step < size]
    return lax.ppermute(array, axis, pairs)


def with_halo(array, axis, dim, width, periodic):
    length = array.shape[dim]
    last = lax.slice_in_dim(array, length - width, length, axis=dim)
    leading = lax.slice_in_dim(array, 0, width, axis=dim)
    before = shift(last, axis, 1, periodic)
    after = shift(leading, axis, -1, periodic)
    return jnp.concatenate([before, array, after], axis=dim)


def weight_table(start, weights, extent, wrapped):
    positions = jnp.arange(extent, dtype=jnp.int32)[:, None]
    table = jnp.zeros((extent, start.shape[0]), jnp.float32)
    for offset in range(4):
        target_cell = start + offset
        if wrapped:
            target_cell = target_cell % extent
        table = table + weights[offset][None, :] * (positions == target_cell[None, :]).astype(
            jnp.float32
        )
    return table


def tables(start_x, start_y, start_z, weights, span_x, span_y, extent_z):
    return (
        weight_table(start_x, weights[0:4], span_x + 4, False),
        weight_table(start_y, weights[4:8], span_y + 4, False),
        weight_table(start_z, weights[8:12], extent_z, True),
    )


def sample_field(field, table_x, table_y, table_z):
    extent_z = field.shape[3]
    partial_z = jnp.dot(field.reshape(-1, extent_z), table_z, precision=lax.Precision.HIGH)
    partial_z = partial_z.reshape(3, field.shape[1], field.shape[2], -1)
    partial_y = jnp.sum(partial_z * table_y[None, None, :, :], axis=2)
    return jnp.sum(partial_y * table_x[None, :, :], axis=1)


def deposit_field(forces, table_x, table_y, table_z):
    spread_xy = forces[:, None, None, :] * table_x[None, :, None, :] * table_y[None, None, :, :]
    count = forces.shape[1]
    flat = lax.dot_general(
        spread_xy.reshape(-1, count),
        table_z,
        (((1,), (1,)), ((), ())),
        precision=lax.Precision.HIGH,
    )
    return flat.reshape(3, table_x.shape[0], table_y.shape[0], table_z.shape[0])


def relax_kernel(e_ref, below_ref, above_ref, mask_ref, out_ref, rhs, one, two):
    span_x, span_y = out_ref.shape[1], out_ref.shape[2]
    wide_x, wide_y = span_x + 2 * ITERS, span_y + 2 * ITERS
    rim = below_ref.shape[2]
    mask = mask_ref[...]
    extent_z = mask.shape[1]

    def build(x, carry):
        one[x] = jnp.zeros((wide_y, extent_z), jnp.float32)
        one[x, 2 : wide_y - 2] = e_ref[0, x]
        one[x, 0:rim] = one[x, 0:rim] + below_ref[0, x]
        one[x, wide_y - rim : wide_y] = one[x, wide_y - rim : wide_y] + above_ref[0, x]
        rhs[x] = one[x] * mask
        return carry

    lax.fori_loop(0, wide_x, build, 0)
    inverse = 1.0 / (1.0 + 6.0 * DIFFUSION)

    def row(source, x):
        here = source[x]
        beside = source[x - 1] + source[x + 1]
        beside = beside + pltpu.roll(here, 1, 0) + pltpu.roll(here, wide_y - 1, 0)
        beside = beside + pltpu.roll(here, 1, 1) + pltpu.roll(here, extent_z - 1, 1)
        return (rhs[x] + DIFFUSION * beside) * (inverse * mask)

    source = rhs
    for sweep in range(ITERS - 1):
        target = one if sweep % 2 == 0 else two

        def step(pair, carry, source=source, target=target, first=sweep + 1):
            x = first + 2 * pair
            new = (row(source, x), row(source, x + 1))
            target[x] = new[0]
            target[x + 1] = new[1]
            return carry

        lax.fori_loop(0, wide_x // 2 - sweep - 1, step, 0)
        source = target

    def last(pair, carry, source=source):
        x = 2 * pair
        new = (row(source, x + ITERS), row(source, x + ITERS + 1))
        out_ref[0, x] = new[0][ITERS : ITERS + span_y]
        out_ref[0, x + 1] = new[1][ITERS : ITERS + span_y]
        return carry

    lax.fori_loop(0, span_x // 2, last, 0)


def relax_all(grown, below, above, mask, span_x, span_y):
    extent_z = grown.shape[3]
    wide = (span_x + 2 * ITERS, span_y + 2 * ITERS, extent_z)

    def block(array):
        return pl.BlockSpec((1,) + array.shape[1:], lambda c: (c, 0, 0, 0))

    return pl.pallas_call(
        relax_kernel,
        grid=(grown.shape[0],),
        out_shape=jax.ShapeDtypeStruct((grown.shape[0], span_x, span_y, extent_z), jnp.float32),
        in_specs=[
            block(grown),
            block(below),
            block(above),
            pl.BlockSpec(mask.shape, lambda c: (0, 0)),
        ],
        out_specs=pl.BlockSpec((1, span_x, span_y, extent_z), lambda c: (c, 0, 0, 0)),
        scratch_shapes=[pltpu.VMEM(wide, jnp.float32)] * 3,
        cost_estimate=pl.CostEstimate(
            flops=40 * grown.size, bytes_accessed=12 * grown.size, transcendentals=0
        ),
        name="relax",
    )(grown, below, above, mask)


def gather_kernel(columns, rows, x_ref, out_ref, held, local_sem, row_send, row_recv, col_send, col_recv):
    column = lax.axis_index("gx")
    row = lax.axis_index("gy")
    row_peers = [lax.rem(row + k, rows) for k in range(1, rows)]
    column_peers = [lax.rem(column + k, columns) for k in range(1, columns)]
    barrier = pltpu.get_barrier_semaphore()
    mesh = pl.DeviceIdType.MESH
    for peer in row_peers:
        pl.semaphore_signal(barrier, inc=1, device_id=(column, peer), device_id_type=mesh)
    for peer in column_peers:
        pl.semaphore_signal(barrier, inc=1, device_id=(peer, row), device_id_type=mesh)
    own = pltpu.make_async_copy(x_ref, held.at[column, row], local_sem)
    own.start()
    pl.semaphore_wait(barrier, rows + columns - 2)
    first = []
    for k, peer in enumerate(row_peers):
        copy = pltpu.make_async_remote_copy(
            src_ref=x_ref,
            dst_ref=held.at[column, row],
            send_sem=row_send.at[k],
            recv_sem=row_recv.at[k],
            device_id=(column, peer),
            device_id_type=mesh,
        )
        copy.start()
        first.append(copy)
    own.wait()
    for copy in first:
        copy.wait()
    second = []
    for k, peer in enumerate(column_peers):
        copy = pltpu.make_async_remote_copy(
            src_ref=held.at[column],
            dst_ref=held.at[column],
            send_sem=col_send.at[k],
            recv_sem=col_recv.at[k],
            device_id=(peer, row),
            device_id_type=mesh,
        )
        copy.start()
        second.append(copy)
    for copy in second:
        copy.wait()
    out_ref[...] = held[...]


def gather_tiles(tile):
    columns, rows = lax.axis_size("gx"), lax.axis_size("gy")
    shape = (columns, rows) + tile.shape
    return pl.pallas_call(
        functools.partial(gather_kernel, columns, rows),
        out_shape=jax.ShapeDtypeStruct(shape, jnp.float32),
        in_specs=[pl.BlockSpec(memory_space=pltpu.VMEM)],
        out_specs=pl.BlockSpec(memory_space=pltpu.VMEM),
        scratch_shapes=[
            pltpu.VMEM(shape, jnp.float32),
            pltpu.SemaphoreType.DMA,
            pltpu.SemaphoreType.DMA((rows - 1,)),
            pltpu.SemaphoreType.DMA((rows - 1,)),
            pltpu.SemaphoreType.DMA((columns - 1,)),
            pltpu.SemaphoreType.DMA((columns - 1,)),
        ],
        compiler_params=pltpu.CompilerParams(collective_id=0, has_side_effects=True),
        cost_estimate=pl.CostEstimate(flops=0, bytes_accessed=40_000_000, transcendentals=0),
        name="gather_tiles",
    )(tile)


ARRIVALS = ((0, 0), (1, 0), (2, 0), (0, 1), (2, 1), (0, 2), (1, 2), (2, 2), (1, 1))


def combine_matrix(columns, rows, per_sphere):
    matrix = np.zeros((columns, rows, columns, rows, TILE_ROWS), np.float32)
    for i in range(columns):
        for j in range(rows):
            for slot, (a, b) in enumerate(ARRIVALS):
                target_row = j + b - 1
                if 0 <= target_row < rows:
                    matrix[(i + a - 1) % columns, target_row, i, j, slot] -= RESPONSE / per_sphere
            matrix[i, j, i, j, len(ARRIVALS)] = 1.0
    return matrix.reshape(columns * rows, -1)


def moments(forces, offsets):
    return jnp.concatenate([forces, jnp.cross(offsets, forces, axis=0)], axis=0)


def on_device(
    velocity,
    owner_block,
    base_x,
    base_y,
    base_z,
    delta_weights,
    marker_offset,
    sphere_motion,
    contact_sphere,
    contact_partner,
):
    span_x = velocity.shape[1]
    span_y = velocity.shape[2]
    extent_z = velocity.shape[3]
    row_count = lax.axis_size("gy")
    column_count = lax.axis_size("gx")
    here = lax.axis_index(("gx", "gy"))
    row_index = lax.axis_index("gy")
    column_index = lax.axis_index("gx")
    grown_field = with_halo(velocity, "gx", 1, 2, True)
    grown_field = with_halo(grown_field, "gy", 2, 2, False)
    markers = base_x.shape[0]
    spheres_here = sphere_motion.shape[1]
    per_sphere = markers // spheres_here
    capacity = markers // 8
    owner = owner_block[:, 0]
    at_home = owner == here
    home_weight = at_home.astype(jnp.float32)
    lanes = 8
    step_x = (owner // row_count - column_index + 1 + column_count) % column_count
    step_y = owner % row_count - row_index + 1
    lane = step_x * 3 + step_y
    lane = lane - (lane > 4).astype(jnp.int32)
    hits = (lane[:, None] == jnp.arange(lanes, dtype=jnp.int32)[None, :]).astype(jnp.int32)
    hits = hits * (1 - at_home.astype(jnp.int32))[:, None]
    ranked = jnp.sum((jnp.cumsum(hits, axis=0) - hits) * hits, axis=1)
    total_slots = lanes * capacity
    slots = jnp.where(at_home, total_slots, lane * capacity + ranked)
    marker_motion = jnp.broadcast_to(
        sphere_motion[:, :, None], (6, spheres_here, per_sphere)
    ).reshape(6, markers)
    target = marker_motion[0:3] + jnp.cross(marker_motion[3:6], marker_offset, axis=0)
    coords = jnp.stack([base_x, base_y, base_z]).astype(jnp.float32)
    sphere_of = (jnp.arange(markers, dtype=jnp.int32) // per_sphere).astype(jnp.float32)
    payload = jnp.concatenate(
        [delta_weights, coords, target, marker_offset, sphere_of[None, :]], axis=0
    )
    outgoing = (
        jnp.zeros((payload.shape[0], total_slots), jnp.float32)
        .at[:, slots]
        .set(payload, mode="drop")
    )
    c = capacity
    from_left = shift(outgoing[:, 5 * c :], "gx", 1, True)
    from_right = shift(outgoing[:, : 3 * c], "gx", -1, True)
    down = [from_left[:, :c], outgoing[:, 3 * c : 4 * c], from_right[:, :c]]
    up = [from_left[:, 2 * c :], outgoing[:, 4 * c : 5 * c], from_right[:, 2 * c :]]
    from_above = shift(jnp.concatenate(down, axis=1), "gy", -1, False)
    from_below = shift(jnp.concatenate(up, axis=1), "gy", 1, False)
    arrived = jnp.concatenate(
        [from_below, from_left[:, c : 2 * c], from_right[:, c : 2 * c], from_above], axis=1
    )

    home_tables = tables(base_x, base_y, base_z, delta_weights, span_x, span_y, extent_z)
    sampled_home = sample_field(grown_field, *home_tables)
    home_force = (target - sampled_home) * home_weight[None, :]
    cell_start = arrived[12:15].astype(jnp.int32)
    slot_tables = tables(
        cell_start[0], cell_start[1], cell_start[2], arrived[0:12], span_x, span_y, extent_z
    )
    slot_force = arrived[15:18] - sample_field(grown_field, *slot_tables)
    forces_all = jnp.concatenate([home_force, slot_force], axis=1)
    all_tables = [jnp.concatenate(pair, axis=1) for pair in zip(home_tables, slot_tables)]
    spread = deposit_field(forces_all, *all_tables)

    spread = spread + jnp.pad(velocity, ((0, 0), (2, 2), (2, 2), (0, 0)))
    reach = ITERS + 2
    left = shift(spread[:, span_x + 4 - reach :], "gx", 1, True)
    right = shift(spread[:, :reach], "gx", -1, True)
    grown = jnp.concatenate(
        [
            left[:, :2],
            spread[:, : reach - 2] + left[:, 2:],
            spread[:, reach - 2 : span_x + 6 - reach],
            spread[:, span_x + 6 - reach :] + right[:, : reach - 2],
            right[:, reach - 2 :],
        ],
        axis=1,
    )
    below = shift(grown[:, :, span_y + 4 - reach :], "gy", 1, False)
    above = shift(grown[:, :, :reach], "gy", -1, False)
    global_row = row_index * span_y - ITERS + jnp.arange(span_y + 2 * ITERS, dtype=jnp.int32)
    inside = jnp.logical_and(global_row >= 0, global_row < span_y * row_count)
    mask = jnp.broadcast_to(inside.astype(jnp.float32)[:, None], (span_y + 2 * ITERS, extent_z))
    state = relax_all(grown, below, above, mask, span_x, span_y)

    home_sums = jnp.sum(
        moments(home_force, marker_offset).reshape(6, spheres_here, per_sphere), axis=-1
    )
    slot_moments = moments(slot_force, arrived[18:21])
    chosen = arrived[21][None, :] == jnp.arange(spheres_here, dtype=jnp.float32)[:, None]
    picked = jnp.where(chosen[None], slot_moments[:, None], 0.0)
    slot_sums = jnp.sum(picked.reshape(6, spheres_here, lanes, capacity), axis=-1)
    columns = jnp.concatenate(
        [slot_sums, home_sums[:, :, None], sphere_motion[:, :, None]], axis=2
    )
    tile = columns.transpose(2, 1, 0).reshape(lanes + 2, spheres_here * 6)
    tile = jnp.pad(tile, ((0, TILE_ROWS - tile.shape[0]), (0, TILE_LANES - tile.shape[1])))
    gathered = gather_tiles(tile).reshape(-1, TILE_LANES)
    matrix = jnp.asarray(combine_matrix(column_count, row_count, per_sphere))
    moved = jnp.dot(matrix, gathered, precision=lax.Precision.HIGHEST)
    moved = moved[:, : spheres_here * 6].reshape(-1, 6)
    all_spheres = jnp.arange(moved.shape[0], dtype=jnp.int32)
    mine = here * spheres_here + jnp.arange(spheres_here, dtype=jnp.int32)
    own = (mine[:, None] == all_spheres[None, :]).astype(jnp.float32)
    acts = (contact_sphere[None, :] == mine[:, None]).astype(jnp.float32)
    partner = (contact_partner[:, None] == all_spheres[None, :]).astype(jnp.float32)
    linked = jnp.sum(acts[:, :, None] * partner[None], axis=1)
    linked = linked - jnp.sum(acts, axis=1)[:, None] * own
    linear_part = jnp.dot(own + DASHPOT * linked, moved[:, :3], precision=lax.Precision.HIGHEST)
    angular_part = jnp.dot(own, moved[:, 3:], precision=lax.Precision.HIGHEST)
    new_motion = jnp.concatenate([linear_part, angular_part], axis=1).T
    return (state, new_motion)


def solution(mesh):
    placed = (
        P(None, "gx", "gy", None),
        P(("gx", "gy"), None),
        P(("gx", "gy")),
        P(("gx", "gy")),
        P(("gx", "gy")),
        P(None, ("gx", "gy")),
        P(None, ("gx", "gy")),
        P(None, ("gx", "gy")),
        P(("gx", "gy")),
        P(("gx", "gy")),
    )
    return jax.shard_map(
        on_device,
        mesh=mesh,
        in_specs=placed,
        out_specs=(P(None, "gx", "gy", None), P(None, ("gx", "gy"))),
        check_vma=False,
    )
```

time: 275 us -> 188 us (0.68)
  the two profiles are of different devices: /device:TPU:0 before, /device:TPU:11 now
where the time goes in v1:
time: 188 us; the launch traced here: 187 us
  matrix products  45 us (24%)
  waiting for transfers between devices  42.2 us (22%)
  Pallas kernels  39.7 us (21%)
  starting transfers between devices  22.4 us (12%)
  local copies, waits for them, and re-layouts  18.9 us (10%)
  other arithmetic  17.9 us (10%)
    ppermute x12, waiting for transfers between devices, shift(): return lax.ppermute(array, axis, pairs)  42.2 us
    dot_general x2, matrix products, sample_field(): jnp.dot(field.reshape(-1, extent_z), table_z, precision=lax.Precision.HIGH)  24.3 us
    pallas_call x1, Pallas kernels, gather_tiles(): pl.pallas_call(functools.partial(gather_kernel, columns, rows), out_shape...  22.9 us
    ppermute x12, starting transfers between devices, shift(): return lax.ppermute(array, axis, pairs)  22.4 us
    dot_general x1, matrix products, deposit_field(): lax.dot_general(spread_xy.reshape(-1, count), table_z, (((1,), (1,)), (()...  19 us
    pallas_call x1, Pallas kernels, relax_all(): pl.pallas_call(relax_kernel, grid=(grown.shape[0],), out_shape=jax.ShapeD...  16.8 us
    scatter x1, local copies, waits for them, and re-layouts, on_device(): outgoing = jnp.zeros((payload.shape[0], total_slots), jnp.float32).at[:,...  5.85 us
    add x5, other arithmetic, weight_table(): table + weights[offset][None, :] * (positions == target_cell[None, :]).as...  4.54 us
  transfers between devices with their start and end apart: 12, of which 7 were waited for; matrix products, arithmetic and copies ran while one was open for 12% of the time, Pallas kernels for 12%

profile of v1, /device:TPU:11, one launch (start us, length us, event | category | flops | bytes accessed | tf_op | source)
XLA Modules:
  0.0 187.3 jit_solution(17616555549506087838)
XLA Ops:
  0.7 1.2 fusion.58
  1.8 1.3 collective-permute-start
  4.9 1.5 fusion.63
  9.7 2.3 %reduce-window.6 = s32[8,16,128]{2,1,0:T(8,128)S(1)} reduce-window(s32[8,16,128]{2,1,0:T(8,128)S(1)} %fusion.17, s32[]{:T(128)} %constant.143.clone.1), window={size=1x1x128 pad=0_0x0_0x127_0}, to_apply=%region_2.4 | reduce-window | flops 2080768 | bytes 131076 | tf_op jit(solution)/shard_map/reduce-window
  17.9 4.3 %collective-permute-start.2 = (f32[3,20,2,256]{3,2,1,0:T(2,128)S(1)}, f32[3,20,2,256]{3,2,1,0:T(2,128)S(1)}, u32[]{:S(2)}, u32[]{:S(2)}) collective-permute-start(f32[3,20,2,256]{3,2,1,0:T(2,128)S(1)} %get-tuple-element.9), channel_id=1, source_target_pairs={{0,1},{1,2},{2,3},{4,5},{5,6},{6,7},{8,9},{9,10},{10,11},{12,13},{... | collective-permute-start | bytes 368648 | tf_op jit(solution)/shard_map/ppermute | solution.py:24
  22.2 1.9 %collective-permute-start.3 = (f32[3,20,2,256]{3,2,1,0:T(2,128)S(1)}, f32[3,20,2,256]{3,2,1,0:T(2,128)S(1)}, u32[]{:S(2)}, u32[]{:S(2)}) collective-permute-start(f32[3,20,2,256]{3,2,1,0:T(2,128)S(1)} %get-tuple-element.10), channel_id=1, source_target_pairs={{1,0},{2,1},{3,2},{5,4},{6,5},{7,6},{9,8},{10,9},{11,10},{13,12},{... | collective-permute-start | bytes 368648 | tf_op jit(solution)/shard_map/ppermute | solution.py:24
  24.4 4.0 %collective-permute-done.3 = f32[3,20,2,256]{3,2,1,0:T(2,128)S(1)} collective-permute-done((f32[3,20,2,256]{3,2,1,0:T(2,128)S(1)}, f32[3,20,2,256]{3,2,1,0:T(2,128)S(1)}, u32[]{:S(2)}, u32[]{:S(2)}) %collective-permute-start.3) | collective-permute-done | bytes 122912 | tf_op jit(solution)/shard_map/ppermute | solution.py:24
  28.4 12.3 %multiply_reduce_fusion.1 = f32[3,20,2048]{2,1,0:T(8,128)S(1)} fusion(f32[36,2048]{1,0:T(8,128)S(1)} %select_add_fusion.3, f32[3,20,2,256]{3,2,1,0:T(2,128)S(1)} %collective-permute-done.3, f32[3,20,32,256]{3,2,1,0:T(8,128)} %copy-done.4, f32[3,20,2,256]{3,2,1,0:T(2,128)S(1)} %collective-permute-done.2, f32[2048]{0:T(1024)S(1)} %bitcast.135, ...), kind=kOutput, calls=%fused_computation.6 | convolution fusion | flops 6810370048 | bytes 3063808 | tf_op jit(solution)/shard_map/dot_general | solution.py:59
  41.5 5.8 %scatter_custom_fusion = f32[22,2048]{0,1:T(8,128)S(1)} fusion(s32[2048]{0:T(1024)S(1)} %bitcast.189, f32[2048,22]{1,0:T(8,128)S(1)} %copy.78, f32[]{:T(128)} %constant.146.clone.1), kind=kCustom, calls=%fused_computation.29 | custom fusion | bytes 180228 | tf_op jit(solution)/shard_map/scatter | solution.py:290
  47.4 0.9 fusion.60
  48.3 2.2 %collective-permute-start.4 = (f32[22,768]{0,1:T(8,128)}, f32[22,768]{0,1:T(8,128)S(1)}, u32[]{:S(2)}, u32[]{:S(2)}) collective-permute-start(f32[22,768]{0,1:T(8,128)} %get-tuple-element.15), channel_id=1, source_target_pairs={{0,4},{4,8},{8,12},{12,16},{16,20},{20,24},{24,28},{28,0},{1,5},{5... | collective-permute-start | bytes 202760 | tf_op jit(solution)/shard_map/ppermute | solution.py:24
  50.7 14.5 %collective-permute-done.4 = f32[22,768]{0,1:T(8,128)S(1)} collective-permute-done((f32[22,768]{0,1:T(8,128)}, f32[22,768]{0,1:T(8,128)S(1)}, u32[]{:S(2)}, u32[]{:S(2)}) %collective-permute-start.4) | collective-permute-done | bytes 67616 | tf_op jit(solution)/shard_map/ppermute | solution.py:24
  65.7 1.9 %collective-permute-start.6 = (f32[22,768]{1,0:T(8,128)S(1)}, f32[22,768]{1,0:T(8,128)S(1)}, u32[]{:S(2)}, u32[]{:S(2)}) collective-permute-start(f32[22,768]{1,0:T(8,128)S(1)} %pad_maximum_fusion.6), channel_id=1, source_target_pairs={{0,1},{1,2},{2,3},{4,5},{5,6},{6,7},{8,9},{9,10},{10,11},{12,13},{... | collective-permute-start | bytes 202760 | tf_op jit(solution)/shard_map/ppermute | solution.py:24
  67.8 2.6 %collective-permute-start.7 = (f32[22,768]{1,0:T(8,128)S(1)}, f32[22,768]{1,0:T(8,128)S(1)}, u32[]{:S(2)}, u32[]{:S(2)}) collective-permute-start(f32[22,768]{1,0:T(8,128)S(1)} %pad_maximum_fusion.7), channel_id=1, source_target_pairs={{1,0},{2,1},{3,2},{5,4},{6,5},{7,6},{9,8},{10,9},{11,10},{13,12},{... | collective-permute-start | bytes 202760 | tf_op jit(solution)/shard_map/ppermute | solution.py:24
  70.9 2.6 %collective-permute-done.7 = f32[22,768]{1,0:T(8,128)S(1)} collective-permute-done((f32[22,768]{1,0:T(8,128)S(1)}, f32[22,768]{1,0:T(8,128)S(1)}, u32[]{:S(2)}, u32[]{:S(2)}) %collective-permute-start.7) | collective-permute-done | bytes 67616 | tf_op jit(solution)/shard_map/ppermute | solution.py:24
  74.1 3.4 %select_add_fusion = (f32[256,2048]{1,0:T(8,128)}, f32[256,2048]{1,0:T(8,128)}) fusion(f32[2048]{0:T(1024)S(1)} %bitcast.143, s32[2048]{0:T(1024)S(1)} %bitcast.151, f32[2048]{0:T(1024)S(1)} %bitcast.145, s32[2048]{0:T(1024)S(1)} %bitcast.153, f32[2048]{0:T(1024)S(1)} %bitcast.147, s32[2048]{0:T(1024)S(1)} %bitcast.155, f32[2048]{0:T(1024)S(1)} %bitcast.149, ...), kind=kLoop, calls=%fused_computation.14 | loop fusion | flops 11534336 | bytes 4325376 | tf_op jit(solution)/shard_map/add | solution.py:43
  77.6 12.0 %multiply_reduce_fusion = f32[3,20,2048]{2,1,0:T(8,128)S(1)} fusion(f32[36,2048]{1,0:T(8,128)S(1)} %select_add_fusion.2, f32[3,20,2,256]{3,2,1,0:T(2,128)S(1)} %copy-done.11, f32[3,20,32,256]{3,2,1,0:T(8,128)S(1)} %copy-done.5, f32[3,20,2,256]{3,2,1,0:T(2,128)S(1)} %collective-permute-done.2, f32[2048]{0:T(1024)S(1)} %bitcast.144, s32[2048]{0:T(1024)S(1)} %bitcast.152, ...), kind=kOutput, calls=%fused_computation.5 | convolution fusion | flops 6810370048 | bytes 3063808 | tf_op jit(solution)/shard_map/dot_general | solution.py:59
  90.0 19.0 %pad_add_fusion = f32[3,20,36,256]{3,2,1,0:T(8,128)S(1)} fusion(f32[3,16,32,256]{3,2,1,0:T(8,128)} %param.13, f32[256,2048]{1,0:T(8,128)} %get-tuple-element.82, f32[256,2048]{1,0:T(8,128)} %get-tuple-element.83, f32[36,4096]{1,0:T(8,128)S(1)} %pad_maximum_fusion.3, f32[3,20,4096]{2,1,0:T(8,128)S(1)} %broadcast_multiply_fusion), kind=kOutput, calls=%fused_computation.11 | convolution fusion | flops 13599993856 | bytes 9551872 | tf_op jit(solution)/shard_map/dot_general | solution.py:68
  109.0 1.0 fusion.56
  110.0 3.0 %collective-permute-start.8 = (f32[3,6,36,256]{3,2,1,0:T(8,128)}, f32[3,6,36,256]{3,2,1,0:T(8,128)}, u32[]{:S(2)}, u32[]{:S(2)}) collective-permute-start(f32[3,6,36,256]{3,2,1,0:T(8,128)} %get-tuple-element.8), channel_id=1, source_target_pairs={{0,4},{4,8},{8,12},{12,16},{16,20},{20,24},{24,28},{28,0},{1,5},{5... | collective-permute-start | bytes 1990664 | tf_op jit(solution)/shard_map/ppermute | solution.py:24
  114.0 22.9 %gather_tiles.1 = f32[8,4,16,128]{3,2,1,0:T(8,128)} custom-call(f32[16,128]{1,0:T(8,128)} %pad.9.x_ref), custom_call_target="tpu_custom_call" | custom-call | bytes 40000000 | tf_op jit(solution)/shard_map/gather_tiles/pallas_call | solution.py:201
  137.0 1.2 fusion.14
  138.7 1.0 slice_dynamic-update-slice_fusion.2
  139.7 1.1 fusion.13
  140.9 15.8 %collective-permute-done.9 = f32[3,6,36,256]{3,2,1,0:T(8,128)S(1)} collective-permute-done((f32[3,6,36,256]{3,2,1,0:T(8,128)S(1)}, f32[3,6,36,256]{3,2,1,0:T(8,128)S(1)}, u32[]{:S(2)}, u32[]{:S(2)}) %collective-permute-start.9) | collective-permute-done | bytes 663584 | tf_op jit(solution)/shard_map/ppermute | solution.py:24
  157.1 1.9 %collective-permute-start.10 = (f32[3,24,6,256]{3,1,2,0:T(8,128)S(1)}, f32[3,24,6,256]{3,1,2,0:T(8,128)S(1)}, u32[]{:S(2)}, u32[]{:S(2)}) collective-permute-start(f32[3,24,6,256]{3,1,2,0:T(8,128)S(1)} %copy.87), channel_id=1, source_target_pairs={{0,1},{1,2},{2,3},{4,5},{5,6},{6,7},{8,9},{9,10},{10,11},{12,13},{... | collective-permute-start | bytes 1327112 | tf_op jit(solution)/shard_map/ppermute | solution.py:24
  159.2 2.6 %collective-permute-start.11 = (f32[3,24,6,256]{3,1,2,0:T(8,128)S(1)}, f32[3,24,6,256]{3,1,2,0:T(8,128)S(1)}, u32[]{:S(2)}, u32[]{:S(2)}) collective-permute-start(f32[3,24,6,256]{3,1,2,0:T(8,128)S(1)} %copy.88), channel_id=1, source_target_pairs={{1,0},{2,1},{3,2},{5,4},{6,5},{7,6},{9,8},{10,9},{11,10},{13,12},{... | collective-permute-start | bytes 1327112 | tf_op jit(solution)/shard_map/ppermute | solution.py:24
  162.9 1.4 collective-permute-done.10
  164.3 1.0 copy.89.below_ref
  165.3 3.6 %collective-permute-done.11 = f32[3,24,6,256]{3,1,2,0:T(8,128)S(1)} collective-permute-done((f32[3,24,6,256]{3,1,2,0:T(8,128)S(1)}, f32[3,24,6,256]{3,1,2,0:T(8,128)S(1)}, u32[]{:S(2)}, u32[]{:S(2)}) %collective-permute-start.11) | collective-permute-done | bytes 442400 | tf_op jit(solution)/shard_map/ppermute | solution.py:24
  168.9 1.0 copy.90.above_ref
  170.5 16.8 %relax.1 = f32[3,16,32,256]{3,2,1,0:T(8,128)} custom-call(f32[3,24,36,256]{3,2,1,0:T(8,128)} %copy-done, f32[3,24,6,256]{3,2,1,0:T(8,128)} %copy.89.below_ref, f32[3,24,6,256]{3,2,1,0:T(8,128)} %copy.90.above_ref, f32[40,256]{1,0:T(8,128)} %broadcast_in_dim.44.mask_ref), custom_call_target="tpu_custom_call" | custom-call | flops 26542080 | bytes 7962624 | tf_op jit(solution)/shard_map/relax/pallas_call | solution.py:133
  (126 shorter events, 17.9 us)
Async XLA Ops:
  0.6 17.0 %copy-start.1 = (f32[3,16,32,256]{3,2,1,0:T(8,128)S(1)}, f32[3,16,32,256]{3,2,1,0:T(8,128)}, u32[]{:S(2)}) copy-start(f32[3,16,32,256]{3,2,1,0:T(8,128)} %param.13) | copy-start | bytes 4718596
  0.6 16.7 %copy-start.6 = (s32[2048]{0:T(1024)S(1)}, s32[2048]{0:T(1024)}, u32[]{:S(2)}) copy-start(s32[2048]{0:T(1024)} %param.15) | copy-start | bytes 24580
  0.7 16.8 %copy-start.9 = (s32[4]{0:T(128)S(1)}, s32[4]{0:T(128)}, u32[]{:S(2)}) copy-start(s32[4]{0:T(128)} %param.21) | copy-start | bytes 52
  1.8 15.7 %collective-permute-start = (f32[3,2,32,256]{3,2,1,0:T(8,128)S(1)}, f32[3,2,32,256]{3,2,1,0:T(8,128)S(1)}, u32[]{:S(2)}, u32[]{:S(2)}) collective-permute-start(f32[3,2,32,256]{3,2,1,0:T(8,128)S(1)} %get-tuple-element.12), channel_id=1, source_target_pairs={{0,4},{4,8},{8,12},{12,16},{16,20},{20,24},{24,28},{28,0},{1,5},{5... | collective-permute-start | bytes 589832 | tf_op jit(solution)/shard_map/ppermute | solution.py:24
  3.2 14.6 %collective-permute-start.1 = (f32[3,2,32,256]{3,2,1,0:T(8,128)S(1)}, f32[3,2,32,256]{3,2,1,0:T(8,128)S(1)}, u32[]{:S(2)}, u32[]{:S(2)}) collective-permute-start(f32[3,2,32,256]{3,2,1,0:T(8,128)S(1)} %get-tuple-element.11), channel_id=1, source_target_pairs={{0,28},{4,0},{8,4},{12,8},{16,12},{20,16},{24,20},{28,24},{1,29},{... | collective-permute-start | bytes 589832 | tf_op jit(solution)/shard_map/ppermute | solution.py:24
  17.6 6.6 %copy-start.8 = (f32[6,2]{0,1:T(2,128)S(1)}, f32[6,2]{0,1:T(2,128)}, u32[]{:S(2)}) copy-start(f32[6,2]{0,1:T(2,128)} %param.20) | copy-start | bytes 148
  17.8 6.3 %copy-start.4 = (f32[3,20,32,256]{3,2,1,0:T(8,128)}, f32[3,20,32,256]{3,2,1,0:T(8,128)S(1)}, u32[]{:S(2)}) copy-start(f32[3,20,32,256]{3,2,1,0:T(8,128)S(1)} %constant_dynamic-update-slice_fusion) | copy-start | bytes 5898244
  17.9 6.4 %collective-permute-start.2 = (f32[3,20,2,256]{3,2,1,0:T(2,128)S(1)}, f32[3,20,2,256]{3,2,1,0:T(2,128)S(1)}, u32[]{:S(2)}, u32[]{:S(2)}) collective-permute-start(f32[3,20,2,256]{3,2,1,0:T(2,128)S(1)} %get-tuple-element.9), channel_id=1, source_target_pairs={{0,1},{1,2},{2,3},{4,5},{5,6},{6,7},{8,9},{9,10},{10,11},{12,13},{... | collective-permute-start | bytes 368648 | tf_op jit(solution)/shard_map/ppermute | solution.py:24
  22.2 6.2 %collective-permute-start.3 = (f32[3,20,2,256]{3,2,1,0:T(2,128)S(1)}, f32[3,20,2,256]{3,2,1,0:T(2,128)S(1)}, u32[]{:S(2)}, u32[]{:S(2)}) collective-permute-start(f32[3,20,2,256]{3,2,1,0:T(2,128)S(1)} %get-tuple-element.10), channel_id=1, source_target_pairs={{1,0},{2,1},{3,2},{5,4},{6,5},{7,6},{9,8},{10,9},{11,10},{13,12},{... | collective-permute-start | bytes 368648 | tf_op jit(solution)/shard_map/ppermute | solution.py:24
  28.4 12.3 %copy-start.10 = (f32[3,20,2,256]{3,2,1,0:T(2,128)}, f32[3,20,2,256]{3,2,1,0:T(2,128)S(1)}, u32[]{:S(2)}) copy-start(f32[3,20,2,256]{3,2,1,0:T(2,128)S(1)} %collective-permute-done.3) | copy-start | bytes 368644
  28.4 12.5 %copy-start.2 = (f32[12,2048]{1,0:T(8,128)S(1)}, f32[12,2048]{1,0:T(8,128)}, u32[]{:S(2)}) copy-start(f32[12,2048]{1,0:T(8,128)} %param.18) | copy-start | bytes 294916
  28.4 12.5 %copy-start.3 = (f32[3,2048]{1,0:T(4,128)S(1)}, f32[3,2048]{1,0:T(4,128)}, u32[]{:S(2)}) copy-start(f32[3,2048]{1,0:T(4,128)} %param.19) | copy-start | bytes 73732
  48.3 17.0 %collective-permute-start.4 = (f32[22,768]{0,1:T(8,128)}, f32[22,768]{0,1:T(8,128)S(1)}, u32[]{:S(2)}, u32[]{:S(2)}) collective-permute-start(f32[22,768]{0,1:T(8,128)} %get-tuple-element.15), channel_id=1, source_target_pairs={{0,4},{4,8},{8,12},{12,16},{16,20},{20,24},{24,28},{28,0},{1,5},{5... | collective-permute-start | bytes 202760 | tf_op jit(solution)/shard_map/ppermute | solution.py:24
  50.5 15.1 %collective-permute-start.5 = (f32[22,768]{0,1:T(8,128)}, f32[22,768]{0,1:T(8,128)S(1)}, u32[]{:S(2)}, u32[]{:S(2)}) collective-permute-start(f32[22,768]{0,1:T(8,128)} %get-tuple-element.16), channel_id=1, source_target_pairs={{0,28},{4,0},{8,4},{12,8},{16,12},{20,16},{24,20},{28,24},{1,29},{... | collective-permute-start | bytes 202760 | tf_op jit(solution)/shard_map/ppermute | solution.py:24
  65.7 5.2 %collective-permute-start.6 = (f32[22,768]{1,0:T(8,128)S(1)}, f32[22,768]{1,0:T(8,128)S(1)}, u32[]{:S(2)}, u32[]{:S(2)}) collective-permute-start(f32[22,768]{1,0:T(8,128)S(1)} %pad_maximum_fusion.6), channel_id=1, source_target_pairs={{0,1},{1,2},{2,3},{4,5},{5,6},{6,7},{8,9},{9,10},{10,11},{12,13},{... | collective-permute-start | bytes 202760 | tf_op jit(solution)/shard_map/ppermute | solution.py:24
  67.8 5.7 %collective-permute-start.7 = (f32[22,768]{1,0:T(8,128)S(1)}, f32[22,768]{1,0:T(8,128)S(1)}, u32[]{:S(2)}, u32[]{:S(2)}) collective-permute-start(f32[22,768]{1,0:T(8,128)S(1)} %pad_maximum_fusion.7), channel_id=1, source_target_pairs={{1,0},{2,1},{3,2},{5,4},{6,5},{7,6},{9,8},{10,9},{11,10},{13,12},{... | collective-permute-start | bytes 202760 | tf_op jit(solution)/shard_map/ppermute | solution.py:24
  74.1 3.5 %copy-start.5 = (f32[3,20,32,256]{3,2,1,0:T(8,128)S(1)}, f32[3,20,32,256]{3,2,1,0:T(8,128)}, u32[]{:S(2)}) copy-start(f32[3,20,32,256]{3,2,1,0:T(8,128)} %copy-done.4) | copy-start | bytes 5898244
  74.1 3.5 %copy-start.11 = (f32[3,20,2,256]{3,2,1,0:T(2,128)S(1)}, f32[3,20,2,256]{3,2,1,0:T(2,128)}, u32[]{:S(2)}) copy-start(f32[3,20,2,256]{3,2,1,0:T(2,128)} %copy-done.10) | copy-start | bytes 368644
  109.0 27.9 %copy-start.7 = (f32[32,512]{1,0:T(8,128)S(1)}, f32[32,512]{1,0:T(8,128)}, u32[]{:S(2)}) copy-start(f32[32,512]{1,0:T(8,128)} %constant.165.clone) | copy-start | bytes 196612
  110.0 28.7 %collective-permute-start.8 = (f32[3,6,36,256]{3,2,1,0:T(8,128)}, f32[3,6,36,256]{3,2,1,0:T(8,128)}, u32[]{:S(2)}, u32[]{:S(2)}) collective-permute-start(f32[3,6,36,256]{3,2,1,0:T(8,128)} %get-tuple-element.8), channel_id=1, source_target_pairs={{0,4},{4,8},{8,12},{12,16},{16,20},{20,24},{24,28},{28,0},{1,5},{5... | collective-permute-start | bytes 1990664 | tf_op jit(solution)/shard_map/ppermute | solution.py:24
  138.2 18.5 %collective-permute-start.9 = (f32[3,6,36,256]{3,2,1,0:T(8,128)S(1)}, f32[3,6,36,256]{3,2,1,0:T(8,128)S(1)}, u32[]{:S(2)}, u32[]{:S(2)}) collective-permute-start(f32[3,6,36,256]{3,2,1,0:T(8,128)S(1)} %get-tuple-element.7), channel_id=1, source_target_pairs={{0,28},{4,0},{8,4},{12,8},{16,12},{20,16},{24,20},{28,24},{1,29},{... | collective-permute-start | bytes 1990664 | tf_op jit(solution)/shard_map/ppermute | solution.py:24
  156.9 2.4 %copy-start = (f32[3,24,36,256]{3,2,1,0:T(8,128)}, f32[3,24,36,256]{3,2,1,0:T(8,128)S(1)}, u32[]{:S(2)}) copy-start(f32[3,24,36,256]{3,2,1,0:T(8,128)S(1)} %slice_dynamic-update-slice_fusion.1.e_ref) | copy-start | bytes 7962628
  157.1 7.2 %collective-permute-start.10 = (f32[3,24,6,256]{3,1,2,0:T(8,128)S(1)}, f32[3,24,6,256]{3,1,2,0:T(8,128)S(1)}, u32[]{:S(2)}, u32[]{:S(2)}) collective-permute-start(f32[3,24,6,256]{3,1,2,0:T(8,128)S(1)} %copy.87), channel_id=1, source_target_pairs={{0,1},{1,2},{2,3},{4,5},{5,6},{6,7},{8,9},{9,10},{10,11},{12,13},{... | collective-permute-start | bytes 1327112 | tf_op jit(solution)/shard_map/ppermute | solution.py:24
  159.2 9.6 %collective-permute-start.11 = (f32[3,24,6,256]{3,1,2,0:T(8,128)S(1)}, f32[3,24,6,256]{3,1,2,0:T(8,128)S(1)}, u32[]{:S(2)}, u32[]{:S(2)}) collective-permute-start(f32[3,24,6,256]{3,1,2,0:T(8,128)S(1)} %copy.88), channel_id=1, source_target_pairs={{1,0},{2,1},{3,2},{5,4},{6,5},{7,6},{9,8},{10,9},{11,10},{13,12},{... | collective-permute-start | bytes 1327112 | tf_op jit(solution)/shard_map/ppermute | solution.py:24
